TPU v7x, 32 devices: a whole 2x2x4 slice. The times are simulated.
32 devices in a mesh: cell: 8 (over y, x, core), narrow: 4 (over z).
Axes of the slice: x: 2, y: 2, z: 4, core: 2. Of those that a mesh axis runs over, the one named last changes fastest.
Arguments:
- snapshots: bfloat16 [4096, 4096], P('cell', 'narrow'), may hold values from -6 to 6
- cell_volume: float32 [4096], P('cell'), may hold values from 0.1 to 10
- mode_vectors: bfloat16 [4096, 512], P('narrow'), may hold values from -0.09375 to 0.09375
- mode_scale: float32 [512], replicated, may hold values from 0.25 to 4
- interp_weights: bfloat16 [4096, 4096], P('cell', 'narrow'), may hold values from -0.09375 to 0.09375
Outputs:
- gram_matrix: float32 [4096, 4096], P('cell', 'narrow')
- fields: bfloat16 [4096, 4096], P('cell', 'narrow')
All inputs are finite; a program needn't handle non-finite values.
Results may differ from a plain program's by a relative error of at most 0.0064.
Values may be sent and summed in bfloat16 or wider, within the bound.
A program may use at most 128 MiB of HBM per device.

v0:
```python
import jax
import jax.numpy as jnp
from jax import lax
from jax.sharding import PartitionSpec as P


def shards(snapshots, cell_volume, mode_vectors, mode_scale, interp_weights):
    total_cells = snapshots.shape[0] * lax.axis_size("cell")
    weighted = (snapshots.astype(jnp.float32) * cell_volume[:, None]).astype(jnp.bfloat16)
    gathered = lax.all_gather(snapshots, "narrow", axis=1, tiled=True)
    gram_block = (
        lax.psum_scatter(
            lax.dot_general(
                gathered, weighted, (((0,), (0,)), ((), ())), preferred_element_type=jnp.float32
            ),
            "cell",
            scatter_dimension=0,
            tiled=True,
        )
        / total_cells
    )
    partial_coeffs = lax.dot_general(
        mode_vectors.astype(jnp.float32),
        gram_block,
        (((0,), (1,)), ((), ())),
        precision=lax.Precision.HIGHEST,
    )
    summed = lax.psum(partial_coeffs, "narrow")
    coefficients = (mode_scale[:, None] * summed).astype(jnp.bfloat16)
    partial_new = jnp.dot(coefficients, interp_weights, preferred_element_type=jnp.float32)
    new_coeffs = lax.psum(partial_new, "cell").astype(jnp.bfloat16)
    partial_shapes = jnp.dot(snapshots, mode_vectors, preferred_element_type=jnp.float32)
    mode_shapes = lax.psum(partial_shapes, "narrow").astype(jnp.bfloat16)
    fields = jnp.dot(mode_shapes, new_coeffs, preferred_element_type=jnp.float32).astype(
        jnp.bfloat16
    )
    return (gram_block, fields)


def solution(mesh):
    return jax.shard_map(
        shards,
        mesh=mesh,
        in_specs=(P("cell", "narrow"), P("cell"), P("narrow", None), P(), P("cell", "narrow")),
        out_specs=(P("cell", "narrow"), P("cell", "narrow")),
        check_vma=False,
    )
```

profile of v0, /device:TPU:25, one launch (start us, length us, event | category | flops | bytes accessed | tf_op | source)
XLA Modules:
  0.0 365.8 jit_solution(10395581222999991774)
XLA Ops:
  7.2 0.0 copy-start
  7.2 0.0 all-gather.2.cloned.1.call-start
  7.2 0.7 all-gather.2.cloned.1.call-update
  7.9 0.0 reduce-scatter.2.cloned.1.call-start
  8.0 80.8 %all-gather.2.cloned.1.call-done = bf16[512,4096]{1,0:T(8,128)(2,1)} async-done(((bf16[512,1024]{1,0:T(8,128)(2,1)}), bf16[512,4096]{1,0:T(8,128)(2,1)}) %all-gather.2.cloned.1.call-update) | async-done | bytes 4194320 | tf_op jit(solution)/shard_map/all_gather | solution.py:10
  88.7 12.9 %convolution_bitcast_fusion = f32[4096,1024]{0,1:T(8,128)} fusion(bf16[512,4096]{1,0:T(8,128)(2,1)} %all-gather.2.cloned.1.call-done, bf16[512,1024]{1,0:T(8,128)(2,1)} %param.5, f32[512]{0:T(512)} %param.6), kind=kOutput, calls=%fused_computation | convolution fusion | flops 4296540160 | bytes 22022144 | tf_op jit(solution)/shard_map/dot_general | solution.py:13
  101.6 0.0 copy-start.2
  101.6 0.0 reduce-scatter.2.cloned.1.call-update
  101.7 0.0 all-reduce.4.cloned.1.call-start
  101.7 0.0 copy-done
  101.7 1.1 copy-done.2
  102.9 1.7 fusion.5
  104.5 114.2 %reduce-scatter.2.cloned.1.call-done = f32[512,1024]{0,1:T(8,128)} async-done(((f32[4096,1024]{0,1:T(8,128)}), f32[512,1024]{0,1:T(8,128)}) %reduce-scatter.2.cloned.1.call-update) | async-done | bytes 2097168 | tf_op jit(solution)/shard_map/reduce_scatter | solution.py:12
  218.7 4.5 %convolution_bitcast_fusion.1 = f32[512,512]{1,0:T(8,128)} fusion(bf16[1024,512]{1,0:T(8,128)(2,1)S(1)} %copy-done, f32[512,1024]{0,1:T(8,128)} %reduce-scatter.2.cloned.1.call-done), kind=kOutput, calls=%fused_computation.3 | convolution fusion | flops 3221749760 | bytes 4194304 | tf_op jit(solution)/shard_map/dot_general | solution.py:22
  223.2 0.0 all-reduce.4.cloned.1.call-update
  223.3 68.1 %all-reduce.6 = bf16[512,512]{1,0:T(8,128)(2,1)} all-reduce(f32[512,512]{1,0:T(8,128)} %fusion.5), channel_id=1, replica_groups=mesh['cell'=8,'narrow'=4] {'narrow'}, use_global_device_ids=true, to_apply=%region_1.0 | all-reduce | flops 262144 | bytes 1572864 | tf_op jit(solution)/shard_map/psum | solution.py:33
  291.4 0.0 copy-done.1
  291.4 1.6 broadcast_multiply_fusion
  293.0 2.9 copy.7
  295.9 2.7 all-reduce.4.cloned.1.call-done
  298.6 0.0 copy-done.3
  298.6 2.3 fusion.2
  300.9 55.3 %all-reduce.5 = bf16[512,1024]{1,0:T(8,128)(2,1)} all-reduce(f32[512,1024]{1,0:T(8,128)S(1)} %fusion.2), channel_id=1, replica_groups=mesh['cell'=8,'narrow'=4] {'cell'}, use_global_device_ids=true, to_apply=%region_3.0 | all-reduce | flops 524288 | bytes 3145728 | tf_op jit(solution)/shard_map/psum | solution.py:31
  356.2 3.1 convolution_convert_fusion
  (2 shorter events, 0.0 us)
Async XLA Ops:
  7.2 94.5 %copy-start = (bf16[1024,512]{1,0:T(8,128)(2,1)S(1)}, bf16[1024,512]{1,0:T(8,128)(2,1)}, u32[]{:S(2)}) copy-start(bf16[1024,512]{1,0:T(8,128)(2,1)} %param.7) | copy-start | bytes 3145732
  7.2 81.6 %all-gather.2.cloned.1.call-start = ((), (), s32[]{:S(2)}) async-start(), calls=%async_computation.1 | async-start | bytes 5242880 | tf_op jit(solution)/shard_map/all_gather | solution.py:10
  7.9 210.8 %reduce-scatter.2.cloned.1.call-start = ((), (), s32[]{:S(2)}) async-start(), calls=%async_computation.2 | async-start | bytes 18874368 | tf_op jit(solution)/shard_map/reduce_scatter | solution.py:12
  101.6 1.2 copy-start.2
  101.7 196.9 %all-reduce.4.cloned.1.call-start = ((), (), s32[]{:S(2)}) async-start(), calls=%async_computation.3 | async-start | bytes 2097152 | tf_op jit(solution)/shard_map/psum | solution.py:28
  223.2 68.2 %copy-start.1 = (f32[512,1024]{0,1:T(8,128)S(1)}, f32[512,1024]{0,1:T(8,128)}, u32[]{:S(2)}) copy-start(f32[512,1024]{0,1:T(8,128)} %reduce-scatter.2.cloned.1.call-done) | copy-start | bytes 6291460
  293.0 5.6 %copy-start.3 = (f32[512]{0:T(512)S(1)}, f32[512]{0:T(512)}, u32[]{:S(2)}) copy-start(f32[512]{0:T(512)} %param.8) | copy-start | bytes 6148
Sparse Core Ops, SparseCore 0:
  9.6 79.1 all-gather.1
  101.8 116.9 reduce-scatter.1
  223.4 75.1 all-reduce.3
where the time goes:
time: 370 us; the launch traced here: 366 us
  waiting for transfers between devices  198 us (54%)
  blocking collectives  123 us (33%)
  matrix products  24.4 us (7%)
  between operations  13.8 us (4%)
  local copies, waits for them, and re-layouts  4.05 us (1%)
    reduce_scatter x1, waiting for transfers between devices, shards(): lax.psum_scatter(lax.dot_general(gathered, weighted, (((0,), (0,)), ((),...  114 us
    all_gather x1, waiting for transfers between devices, shards(): gathered = lax.all_gather(snapshots, 'narrow', axis=1, tiled=True)  80.8 us
    psum x1, blocking collectives, shards(): mode_shapes = lax.psum(partial_shapes, 'narrow').astype(jnp.bfloat16)  68.1 us
    psum x1, blocking collectives, shards(): new_coeffs = lax.psum(partial_new, 'cell').astype(jnp.bfloat16)  55.3 us
    dot_general x1, matrix products, shards(): lax.dot_general(gathered, weighted, (((0,), (0,)), ((), ())), preferred_e...  12.9 us
  transfers between devices with their start and end apart: 3, of which 3 were waited for; matrix products, arithmetic and copies ran while one was open for 2% of the time, Pallas kernels for 0%

commit v1 on v0

v1 whole, which is shorter than its diff:
```python
import jax
import jax.numpy as jnp
from jax import lax
from jax.sharding import PartitionSpec as P


def shards(snapshots, cell_volume, mode_vectors, mode_scale, interp_weights):
    f32, bf16 = jnp.float32, jnp.bfloat16
    n_cell, n_narrow = lax.axis_size("cell"), lax.axis_size("narrow")
    total_cells = snapshots.shape[0] * n_cell
    rows = interp_weights.shape[0]
    weighted = (snapshots.astype(f32) * cell_volume[:, None]).astype(bf16)

    partial_shapes = jnp.dot(snapshots, mode_vectors, preferred_element_type=f32)
    mode_shapes = lax.psum(partial_shapes, "narrow").astype(bf16)

    gathered = lax.all_gather(snapshots, "narrow", axis=1, tiled=True)
    scaled_shapes = (
        mode_shapes.astype(f32) * (cell_volume / total_cells)[:, None] * mode_scale[None, :]
    ).astype(bf16)
    partial_coeffs = lax.dot_general(
        gathered, scaled_shapes, (((0,), (0,)), ((), ())), preferred_element_type=f32
    ).astype(bf16)
    coeffs = lax.psum_scatter(partial_coeffs, "cell", scatter_dimension=0, tiled=True)
    partial_new = lax.dot_general(
        coeffs, interp_weights, (((0,), (0,)), ((), ())), preferred_element_type=f32
    )
    new_coeffs = lax.psum(partial_new, "cell").astype(bf16)
    fields = jnp.dot(mode_shapes, new_coeffs, preferred_element_type=f32).astype(bf16)

    partial_gram = (
        lax.dot_general(gathered, weighted, (((0,), (0,)), ((), ())), preferred_element_type=f32)
        / total_cells
    ).astype(bf16)
    gram = lax.psum_scatter(partial_gram, "cell", scatter_dimension=0, tiled=True)
    return (gram.astype(f32), fields)


def solution(mesh):
    return jax.shard_map(
        shards,
        mesh=mesh,
        in_specs=(P("cell", "narrow"), P("cell"), P("narrow", None), P(), P("cell", "narrow")),
        out_specs=(P("cell", "narrow"), P("cell", "narrow")),
        check_vma=False,
    )
```

time: 370 us -> 282 us (0.76)
  waiting for transfers between devices: 198 us -> 100 us
  blocking collectives: 123 us -> 139 us
    reduce_scatter x1 -> x2, waiting for transfers between devices: 114 us -> 60.1 us  [the longest x1 41.5 us: shards(): lax.psum_scatter(partial_coeffs, 'cell', scatter_dimension=0, tiled=True)]
    all_gather x1, waiting for transfers between devices: 80.8 us -> 39.3 us  [shards(): gathered = lax.all_gather(snapshots, 'narrow', axis=1, tiled=True)]
    psum x2, blocking collectives: 123 us -> 139 us  [the longest x1 71.2 us: shards(): new_coeffs = lax.psum(partial_new, 'cell').astype(bf16)]
    dot_general x1, matrix products: 12.9 us -> 9.13 us  [shards(): lax.dot_general(gathered, weighted, (((0,), (0,)), ((), ())), preferred_e...]
  transfers between devices with their start and end apart: 3 -> 3, of which waited for: 3 -> 3; matrix products, arithmetic and copies ran while one was open for 2% -> 6% of each run, Pallas kernels for 0% -> 0%
where the time goes in v1:
time: 282 us; the launch traced here: 280 us
  blocking collectives  139 us (49%)
  waiting for transfers between devices  100 us (35%)
  matrix products  22.8 us (8%)
  between operations  13.8 us (5%)
  local copies, waits for them, and re-layouts  3.74 us (1%)
    psum x1, blocking collectives, shards(): new_coeffs = lax.psum(partial_new, 'cell').astype(bf16)  71.2 us
    psum x1, blocking collectives, shards(): mode_shapes = lax.psum(partial_shapes, 'narrow').astype(bf16)  67.8 us
    reduce_scatter x1, waiting for transfers between devices, shards(): lax.psum_scatter(partial_coeffs, 'cell', scatter_dimension=0, tiled=True)  41.5 us
    all_gather x1, waiting for transfers between devices, shards(): gathered = lax.all_gather(snapshots, 'narrow', axis=1, tiled=True)  39.3 us
    reduce_scatter x1, waiting for transfers between devices, shards(): lax.psum_scatter(partial_gram, 'cell', scatter_dimension=0, tiled=True)  18.7 us
    dot_general x1, matrix products, shards(): lax.dot_general(gathered, weighted, (((0,), (0,)), ((), ())), preferred_e...  9.13 us
    dot_general x1, matrix products, shards(): lax.dot_general(gathered, scaled_shapes, (((0,), (0,)), ((), ())), prefer...  6.61 us
  transfers between devices with their start and end apart: 3, of which 3 were waited for; matrix products, arithmetic and copies ran while one was open for 6% of the time, Pallas kernels for 0%

profile of v1, /device:TPU:25, one launch (start us, length us, event | category | flops | bytes accessed | tf_op | source)
XLA Modules:
  0.0 279.6 jit_solution(1832069264775600661)
XLA Ops:
  7.2 0.0 copy-start
  7.2 0.0 copy-start.4
  7.2 0.0 copy-start.3
  7.2 0.0 all-gather.2.cloned.1.call-start
  7.2 0.7 all-gather.2.cloned.1.call-update
  7.9 0.0 reduce-scatter.5.cloned.1.call-start
  8.0 2.2 fusion.8
  10.2 0.0 copy-done.4
  10.3 67.8 %all-reduce.2 = bf16[512,512]{1,0:T(8,128)(2,1)S(1)} all-reduce(f32[512,512]{1,0:T(8,128)S(1)} %fusion.8), channel_id=1, replica_groups=mesh['cell'=8,'narrow'=4] {'narrow'}, use_global_device_ids=true, to_apply=%region_1.0 | all-reduce | flops 262144 | bytes 1572864 | tf_op jit(solution)/shard_map/psum | solution.py:15
  78.0 0.0 copy-start.1
  78.0 39.3 %all-gather.2.cloned.1.call-done = bf16[512,4096]{1,0:T(8,128)(2,1)} async-done(((bf16[512,1024]{1,0:T(8,128)(2,1)}), bf16[512,4096]{1,0:T(8,128)(2,1)}) %all-gather.2.cloned.1.call-update) | async-done | bytes 4194320 | tf_op jit(solution)/shard_map/all_gather | solution.py:17
  117.4 0.0 copy-done.3
  117.4 6.6 %fusion.1 = bf16[4096,512]{0,1:T(8,128)(2,1)} fusion(bf16[512,4096]{1,0:T(8,128)(2,1)} %all-gather.2.cloned.1.call-done, f32[512]{0:T(512)S(1)} %copy-done.3, f32[512]{0:T(512)S(1)} %broadcast_multiply_fusion, bf16[512,512]{1,0:T(8,128)(2,1)S(1)} %all-reduce.2), kind=kOutput, calls=%fused_computation.3 | convolution fusion | flops 2150629376 | bytes 8916992 | tf_op jit(solution)/shard_map/dot_general | solution.py:21
  124.0 0.0 reduce-scatter.5.cloned.1.call-update
  124.0 0.0 reduce-scatter.3.cloned.1.call-start
  124.1 1.1 copy-done.2
  125.2 9.1 %fusion = bf16[4096,1024]{0,1:T(8,128)(2,1)} fusion(bf16[512,4096]{1,0:T(8,128)(2,1)} %all-gather.2.cloned.1.call-done, bf16[512,1024]{1,0:T(8,128)(2,1)S(1)} %copy-done.2, f32[512]{0:T(512)S(1)} %copy-done.4), kind=kOutput, calls=%fused_computation.1 | convolution fusion | flops 4304928768 | bytes 13633536 | tf_op jit(solution)/shard_map/dot_general | solution.py:32
  134.4 0.0 reduce-scatter.3.cloned.1.call-update
  134.4 41.5 %reduce-scatter.5.cloned.1.call-done = bf16[512,512]{0,1:T(8,128)(2,1)} async-done(((bf16[4096,512]{0,1:T(8,128)(2,1)}), bf16[512,512]{0,1:T(8,128)(2,1)}) %reduce-scatter.5.cloned.1.call-update) | async-done | bytes 524304 | tf_op jit(solution)/shard_map/reduce_scatter | solution.py:24
  175.9 1.8 fusion.9
  177.6 71.2 %all-reduce.3 = bf16[512,1024]{1,0:T(8,128)(2,1)} all-reduce(f32[512,1024]{1,0:T(8,128)S(1)} %fusion.9), channel_id=1, replica_groups=mesh['cell'=8,'narrow'=4] {'cell'}, use_global_device_ids=true, to_apply=%region_3.0 | all-reduce | flops 524288 | bytes 3145728 | tf_op jit(solution)/shard_map/psum | solution.py:28
  248.8 3.1 %convolution_convert_fusion.1 = bf16[512,1024]{1,0:T(8,128)(2,1)} fusion(bf16[512,1024]{1,0:T(8,128)(2,1)} %all-reduce.3, bf16[512,512]{1,0:T(8,128)(2,1)} %copy-done.1), kind=kOutput, calls=%fused_computation.5 | convolution fusion | flops 537395200 | bytes 2621440 | tf_op jit(solution)/shard_map/dot_general | solution.py:29
  251.9 18.7 %reduce-scatter.3.cloned.1.call-done = bf16[512,1024]{0,1:T(8,128)(2,1)} async-done(((bf16[4096,1024]{0,1:T(8,128)(2,1)}), bf16[512,1024]{0,1:T(8,128)(2,1)}) %reduce-scatter.3.cloned.1.call-update) | async-done | bytes 1048592 | tf_op jit(solution)/shard_map/reduce_scatter | solution.py:35
  270.5 2.6 copy.7
  (4 shorter events, 0.0 us)
Async XLA Ops:
  7.2 168.7 %copy-start = (bf16[512,1024]{1,0:T(8,128)(2,1)S(1)}, bf16[512,1024]{1,0:T(8,128)(2,1)}, u32[]{:S(2)}) copy-start(bf16[512,1024]{1,0:T(8,128)(2,1)} %param.9) | copy-start | bytes 3145732
  7.2 3.1 %copy-start.4 = (f32[512]{0:T(512)S(1)}, f32[512]{0:T(512)}, u32[]{:S(2)}) copy-start(f32[512]{0:T(512)} %param.6) | copy-start | bytes 6148
  7.2 110.2 %copy-start.3 = (f32[512]{0:T(512)S(1)}, f32[512]{0:T(512)}, u32[]{:S(2)}) copy-start(f32[512]{0:T(512)} %param.8) | copy-start | bytes 6148
  7.2 110.2 %all-gather.2.cloned.1.call-start = ((), (), s32[]{:S(2)}) async-start(), calls=%async_computation.2 | async-start | bytes 5242880 | tf_op jit(solution)/shard_map/all_gather | solution.py:17
  7.9 167.9 %reduce-scatter.5.cloned.1.call-start = ((), (), s32[]{:S(2)}) async-start(), calls=%async_computation.4 | async-start | bytes 4718592 | tf_op jit(solution)/shard_map/reduce_scatter | solution.py:24
  78.0 46.0 %copy-start.1 = (bf16[512,512]{1,0:T(8,128)(2,1)}, bf16[512,512]{1,0:T(8,128)(2,1)S(1)}, u32[]{:S(2)}) copy-start(bf16[512,512]{1,0:T(8,128)(2,1)S(1)} %all-reduce.2) | copy-start | bytes 1572868
  124.0 1.2 copy-start.2
  124.0 146.5 %reduce-scatter.3.cloned.1.call-start = ((), (), s32[]{:S(2)}) async-start(), calls=%async_computation.3 | async-start | bytes 9437184 | tf_op jit(solution)/shard_map/reduce_scatter | solution.py:35
Sparse Core Ops, SparseCore 0:
  9.6 107.7 all-gather.1
  124.2 51.6 reduce-scatter.4
  179.3 91.1 reduce-scatter.2

commit v2 on v1

--- a/solution.py
+++ b/solution.py
@@ -1,10 +1,18 @@
+import functools
+
 import jax
 import jax.numpy as jnp
 from jax import lax
+from jax.experimental import pallas as pl
+from jax.experimental.pallas import tpu as pltpu
 from jax.sharding import PartitionSpec as P
 
-
-def shards(snapshots, cell_volume, mode_vectors, mode_scale, interp_weights):
+F32, BF16 = jnp.float32, jnp.bfloat16
+MESH = pl.DeviceIdType.MESH
+CHUNKS = 4
+
+
+def shards_xla(snapshots, cell_volume, mode_vectors, mode_scale, interp_weights):
     f32, bf16 = jnp.float32, jnp.bfloat16
     n_cell, n_narrow = lax.axis_size("cell"), lax.axis_size("narrow")
     total_cells = snapshots.shape[0] * n_cell
@@ -36,6 +44,383 @@
     return (gram.astype(f32), fields)
 
 
+def kernel(
+    C, Z, total, s, volb, v, scale, w, gram, fields,
+    sg, sp, volp, wf, gsend, grecv, mpart, mrecv, mg, mgp, dm, csend, crecv, cb, ksend, krecv, kg,
+    loc_sem, ps_sem, pr_sem, xs_sem, xr_sem, zs_sem, zr_sem, gs_sem, gr_sem,
+    ms_sem, mr_sem, as_sem, ar_sem, cs_sem, cr_sem, bs_sem, br_sem,
+    ks_sem, kr_sem, ls_sem, lr_sem,
+):
+    c, z = lax.axis_index("cell"), lax.axis_index("narrow")
+    groups = C // 2
+    p, k = lax.div(c, 2), lax.rem(c, 2)
+    mate = 2 * p + 1 - k
+    rows, cols = s.shape
+    modes = v.shape[1]
+    half = cols // 2
+    cw = half // CHUNKS
+    mrows = rows // Z
+    krows = modes // C
+
+    def remote(src, dst, ssem, rsem, cell, narrow):
+        return pltpu.make_async_remote_copy(
+            src_ref=src, dst_ref=dst, send_sem=ssem, recv_sem=rsem,
+            device_id={"cell": cell, "narrow": narrow}, device_id_type=MESH,
+        )
+
+    def other(me, step, n):
+        return lax.rem(me + step, n)
+
+    barrier = pltpu.get_barrier_semaphore()
+    for d in range(1, C):
+        pl.semaphore_signal(
+            barrier, inc=1, device_id={"cell": other(c, d, C), "narrow": z}, device_id_type=MESH
+        )
+    for d in range(1, Z):
+        pl.semaphore_signal(
+            barrier, inc=1, device_id={"cell": c, "narrow": other(z, d, Z)}, device_id_type=MESH
+        )
+    pl.semaphore_wait(barrier, C + Z - 2)
+
+    mine = pl.ds(pl.multiple_of(k * rows, rows), rows)
+    theirs = pl.ds(pl.multiple_of((1 - k) * rows, rows), rows)
+
+    def local_copy(h):
+        lanes = pl.ds(pl.multiple_of(k * half + h * cw, cw), cw)
+        return pltpu.make_async_copy(s.at[:, lanes], sg.at[z, h, mine], loc_sem.at[h])
+
+    def mate_copy(h):
+        lanes = pl.ds(pl.multiple_of((1 - k) * half + h * cw, cw), cw)
+        return remote(
+            s.at[:, lanes], sg.at[z, h, mine], ps_sem.at[h], pr_sem.at[h], mate, z
+        )
+
+    block_copy = remote(s, sp, xs_sem.at[0], xr_sem.at[0], mate, z)
+    vol_copy = remote(volb, volp, xs_sem.at[1], xr_sem.at[1], mate, z)
+    for h in range(CHUNKS):
+        local_copy(h).start()
+        mate_copy(h).start()
+    vol_copy.start()
+    block_copy.start()
+
+    mpart[...] = jnp.dot(s[...], v[...], preferred_element_type=F32)
+
+    def shape_rows(b):
+        return pl.ds(pl.multiple_of(b * mrows, mrows), mrows)
+
+    def shape_send(d):
+        t = other(z, d, Z)
+        return remote(mpart.at[shape_rows(t)], mrecv.at[z], ms_sem.at[t], mr_sem.at[z], c, t)
+
+    for d in range(1, Z):
+        shape_send(d).start()
+
+    def chain(side, b, h):
+        to = jnp.minimum(z + 1, Z - 1) if side == 0 else jnp.maximum(z - 1, 0)
+        return remote(sg.at[b, h], sg.at[b, h], zs_sem.at[side, b, h], zr_sem.at[b, h], c, to)
+
+    for h in range(CHUNKS):
+        local_copy(h).wait()
+        mate_copy(h).wait_recv()
+
+        @pl.when(z < Z - 1)
+        def _():
+            chain(0, z, h).start()
+
+        @pl.when(z > 0)
+        def _():
+            chain(1, z, h).start()
+
+    wf[mine, :] = (s[...].astype(F32) * volb[:, :1]).astype(BF16)
+    vol_copy.wait_recv()
+    block_copy.wait_recv()
+    wf[theirs, :] = (sp[...].astype(F32) * volp[:, :1]).astype(BF16)
+
+    def gram_send(b, h):
+        return remote(
+            gsend.at[b, h], grecv.at[p, h], gs_sem.at[b, h], gr_sem.at[p, h], 2 * b + k, z
+        )
+
+    def gram_term(b, h):
+        term = lax.dot_general(
+            sg[b, h], wf[...], (((0,), (0,)), ((), ())), preferred_element_type=F32
+        ) * (1.0 / total)
+
+        @pl.when(b == p)
+        def _():
+            gram[pl.ds(pl.multiple_of(h * cw, cw), cw), :] = term
+
+        @pl.when(b != p)
+        def _():
+            gsend[b, h] = term.astype(BF16)
+            gram_send(b, h).start()
+
+    @pl.loop(0, CHUNKS)
+    def _(h):
+        gram_term(z, h)
+
+    acc = mpart[shape_rows(z), :]
+    for d in range(1, Z):
+        q = other(z, d, Z)
+        remote(mpart.at[shape_rows(z)], mrecv.at[q], ms_sem.at[q], mr_sem.at[q], c, q).wait_recv()
+        acc = acc + mrecv[q]
+    mg[shape_rows(z), :] = acc.astype(BF16)
+
+    def shape_share(d, b):
+        t = other(z, d, Z)
+        return remote(mg.at[shape_rows(b)], mg.at[shape_rows(b)], as_sem.at[t], ar_sem.at[b], c, t)
+
+    for d in range(1, Z):
+        shape_share(d, z).start()
+
+    def hop(t, h):
+        for side in (0, 1):
+            b = z - t if side == 0 else z + t
+            there = b >= 0 if side == 0 else b < Z
+            onward = z < Z - 1 if side == 0 else z > 0
+
+            @pl.when(there)
+            def _():
+                chain(side, b, h).wait_recv()
+
+                @pl.when(onward)
+                def _():
+                    chain(side, b, h).start()
+
+                gram_term(b, h)
+
+    def hops(t):
+        @pl.loop(0, CHUNKS)
+        def _(h):
+            hop(t, h)
+
+    hops(1)
+
+    for d in range(1, Z):
+        shape_share(d, other(z, d, Z)).wait_recv()
+        shape_send(d).wait_send()
+    mate_shapes = remote(mg, mgp, xs_sem.at[2], xr_sem.at[2], mate, z)
+    mate_shapes.start()
+    dm[mine, :] = (mg[...].astype(F32) * volb[:, :1]).astype(BF16)
+    mate_shapes.wait_recv()
+    dm[theirs, :] = (mgp[...].astype(F32) * volp[:, :1]).astype(BF16)
+    diagonal = p == z
+
+    def coeff_send():
+        return remote(csend, crecv.at[p], cs_sem.at[0], cr_sem.at[p], 2 * z + k, z)
+
+    def coeff_share(side):
+        to = jnp.minimum(z + 1, Z - 1) if side == 0 else jnp.maximum(z - 1, 0)
+        return remote(cb, cb, bs_sem.at[side], br_sem.at[0], c, to)
+
+    @pl.loop(0, CHUNKS)
+    def _(h):
+        at = pl.ds(pl.multiple_of(h * cw, cw), cw)
+        term = lax.dot_general(
+            sg[z, h], dm[...], (((0,), (0,)), ((), ())), preferred_element_type=F32
+        )
+
+        @pl.when(diagonal)
+        def _():
+            mpart[at, :] = term
+
+        @pl.when(p != z)
+        def _():
+            csend[at, :] = term.astype(BF16)
+
+    @pl.when(p != z)
+    def _():
+        coeff_send().start()
+
+    if Z > 2:
+        hops(2)
+
+    @pl.when(diagonal)
+    def _():
+        total_c = mpart[...]
+        for d in range(1, groups):
+            q = other(p, d, groups)
+            remote(
+                csend, crecv.at[q], cs_sem.at[0], cr_sem.at[q], 2 * q + k, z
+            ).wait_recv()
+            total_c = total_c + crecv[q].astype(F32)
+        cb[...] = (total_c * (scale[...] * (1.0 / total))).astype(BF16)
+
+        @pl.when(z < Z - 1)
+        def _():
+            coeff_share(0).start()
+
+        @pl.when(z > 0)
+        def _():
+            coeff_share(1).start()
+
+    @pl.when(z > p)
+    def _():
+        coeff_share(0).wait_recv()
+
+        @pl.when(z < Z - 1)
+        def _():
+            coeff_share(0).start()
+
+    @pl.when(z < p)
+    def _():
+        coeff_share(1).wait_recv()
+
+        @pl.when(z > 0)
+        def _():
+            coeff_share(1).start()
+
+    def new_send(t):
+        return remote(ksend.at[t], krecv.at[c], ks_sem.at[t], kr_sem.at[c], t, z)
+
+    part = lax.dot_general(cb[...], w[...], (((0,), (0,)), ((), ())), preferred_element_type=F32)
+    ksend[...] = part.reshape(C, krows, w.shape[1]).astype(BF16)
+    for d in range(1, C):
+        new_send(other(c, d, C)).start()
+
+    for t in range(3, Z):
+        hops(t)
+
+    new = ksend[c].astype(F32)
+    for d in range(1, C):
+        q = other(c, d, C)
+        remote(ksend.at[q], krecv.at[q], ks_sem.at[q], kr_sem.at[q], q, z).wait_recv()
+        new = new + krecv[q].astype(F32)
+    kg[c] = new.astype(BF16)
+
+    def new_share(t, b):
+        return remote(kg.at[b], kg.at[b], ls_sem.at[t], lr_sem.at[b], t, z)
+
+    for d in range(1, C):
+        new_share(other(c, d, C), c).start()
+
+    @pl.loop(0, CHUNKS)
+    def _(h):
+        at = pl.ds(pl.multiple_of(h * cw, cw), cw)
+        acc = gram[at, :]
+        for d in range(1, groups):
+            q = other(p, d, groups)
+            remote(
+                gsend.at[q, h], grecv.at[q, h], gs_sem.at[q, h], gr_sem.at[q, h], 2 * q + k, z
+            ).wait_recv()
+            acc = acc + grecv[q, h].astype(F32)
+        gram[at, :] = acc
+
+    for d in range(1, C):
+        q = other(c, d, C)
+        new_share(q, q).wait_recv()
+    fields[...] = jnp.dot(
+        mg[...], kg[...].reshape(modes, w.shape[1]), preferred_element_type=F32
+    ).astype(BF16)
+
+    vol_copy.wait_send()
+    block_copy.wait_send()
+    mate_shapes.wait_send()
+    for h in range(CHUNKS):
+        mate_copy(h).wait_send()
+    for d in range(1, Z):
+        shape_share(d, z).wait_send()
+    for d in range(1, C):
+        new_send(other(c, d, C)).wait_send()
+        new_share(other(c, d, C), c).wait_send()
+
+    @pl.when(p != z)
+    def _():
+        coeff_send().wait_send()
+
+    @pl.when((z >= p) & (z < Z - 1))
+    def _():
+        coeff_share(0).wait_send()
+
+    @pl.when((z <= p) & (z > 0))
+    def _():
+        coeff_share(1).wait_send()
+
+    @pl.loop(0, CHUNKS)
+    def _(h):
+        for b in range(Z):
+            @pl.when((b <= z) & (z < Z - 1))
+            def _():
+                chain(0, b, h).wait_send()
+
+            @pl.when((b >= z) & (z > 0))
+            def _():
+                chain(1, b, h).wait_send()
+
+        for d in range(1, groups):
+            gram_send(other(p, d, groups), h).wait_send()
+
+
+def shards_kernel(snapshots, cell_volume, mode_vectors, mode_scale, interp_weights):
+    C, Z = lax.axis_size("cell"), lax.axis_size("narrow")
+    groups = C // 2
+    rows, cols = snapshots.shape
+    modes = mode_vectors.shape[1]
+    conds = interp_weights.shape[1]
+    half = cols // 2
+    cw = half // CHUNKS
+    dma = pltpu.SemaphoreType.DMA
+    volb = jnp.broadcast_to(cell_volume[:, None], (rows, 128))
+    vmem = pl.BlockSpec(memory_space=pltpu.VMEM)
+    return pl.pallas_call(
+        functools.partial(kernel, C, Z, rows * C),
+        out_shape=(
+            jax.ShapeDtypeStruct((half, cols), F32),
+            jax.ShapeDtypeStruct((rows, conds), BF16),
+        ),
+        in_specs=[vmem] * 5,
+        out_specs=(vmem, vmem),
+        scratch_shapes=[
+            pltpu.VMEM((Z, CHUNKS, 2 * rows, cw), BF16),
+            pltpu.VMEM((rows, cols), BF16),
+            pltpu.VMEM((rows, 128), F32),
+            pltpu.VMEM((2 * rows, cols), BF16),
+            pltpu.VMEM((groups, CHUNKS, cw, cols), BF16),
+            pltpu.VMEM((groups, CHUNKS, cw, cols), BF16),
+            pltpu.VMEM((rows, modes), F32),
+            pltpu.VMEM((Z, rows // Z, modes), F32),
+            pltpu.VMEM((rows, modes), BF16),
+            pltpu.VMEM((rows, modes), BF16),
+            pltpu.VMEM((2 * rows, modes), BF16),
+            pltpu.VMEM((half, modes), BF16),
+            pltpu.VMEM((groups, half, modes), BF16),
+            pltpu.VMEM((half, modes), BF16),
+            pltpu.VMEM((C, modes // C, conds), BF16),
+            pltpu.VMEM((C, modes // C, conds), BF16),
+            pltpu.VMEM((C, modes // C, conds), BF16),
+            dma((CHUNKS,)), dma((CHUNKS,)), dma((CHUNKS,)),
+            dma((3,)), dma((3,)),
+            dma((2, Z, CHUNKS)), dma((Z, CHUNKS)),
+            dma((groups, CHUNKS)), dma((groups, CHUNKS)),
+            dma((Z,)), dma((Z,)), dma((Z,)), dma((Z,)),
+            dma((1,)), dma((groups,)),
+            dma((2,)), dma((1,)),
+            dma((C,)), dma((C,)), dma((C,)), dma((C,)),
+        ],
+        compiler_params=pltpu.CompilerParams(
+            collective_id=0, has_side_effects=True, vmem_limit_bytes=52 * 1024 * 1024
+        ),
+    )(snapshots, volb, mode_vectors, mode_scale[None, :], interp_weights)
+
+
+def shards(snapshots, cell_volume, mode_vectors, mode_scale, interp_weights):
+    C, Z = lax.axis_size("cell"), lax.axis_size("narrow")
+    rows, cols = snapshots.shape
+    modes = mode_vectors.shape[1]
+    fits = (
+        C == 2 * Z
+        and cols % (2 * 128 * CHUNKS) == 0
+        and rows % (16 * Z) == 0
+        and modes % (16 * C) == 0
+        and interp_weights.shape[0] == rows == cols // 2
+        and rows * cols <= 512 * 1024
+        and interp_weights.shape[1] <= 1024
+        and modes <= 512
+    )
+    run = shards_kernel if fits else shards_xla
+    return run(snapshots, cell_volume, mode_vectors, mode_scale, interp_weights)
+
+
 def solution(mesh):
     return jax.shard_map(
         shards,

time: 282 us -> 177 us (0.63)
  Pallas kernels: 0 us -> 171 us
  blocking collectives: 139 us -> 0 us
  waiting for transfers between devices: 100 us -> 0 us
  matrix products: 22.8 us -> 0 us
  between operations: 13.8 us -> 0.65 us
    pallas_call x0 -> x1, Pallas kernels: none -> 171 us  [shards_kernel(): pl.pallas_call(functools.partial(kernel, C, Z, rows * C), out_shape=(jax....]
    psum x2 -> x0, blocking collectives: 139 us -> none  [the longest x1 71.2 us: shards(): new_coeffs = lax.psum(partial_new, 'cell').astype(bf16)]
    reduce_scatter x2 -> x0, waiting for transfers between devices: 60.1 us -> none  [the longest x1 41.5 us: shards(): lax.psum_scatter(partial_coeffs, 'cell', scatter_dimension=0, tiled=True)]
    all_gather x1 -> x0, waiting for transfers between devices: 39.3 us -> none  [shards(): gathered = lax.all_gather(snapshots, 'narrow', axis=1, tiled=True)]
    dot_general x5 -> x0, matrix products: 22.8 us -> none  [the longest x1 9.13 us: shards(): lax.dot_general(gathered, weighted, (((0,), (0,)), ((), ())), preferred_e...]
  transfers between devices with their start and end apart: 3 -> 0, of which waited for: 3 -> 0; matrix products, arithmetic and copies ran while one was open for 6% -> 0% of each run, Pallas kernels for 0% -> 0%
where the time goes in v2:
time: 177 us
  Pallas kernels  171 us (97%)
  local copies, waits for them, and re-layouts  5.61 us (3%)
    pallas_call x1, Pallas kernels, shards_kernel(): pl.pallas_call(functools.partial(kernel, C, Z, rows * C), out_shape=(jax....  171 us
    unnamed x4, local copies, waits for them, and re-layouts  4.81 us

profile of v2, /device:TPU:25, one launch (start us, length us, event | category | flops | bytes accessed | tf_op | source)
XLA Modules:
  0.0 176.9 jit_solution(14116649267414716662)
XLA Ops:
  0.6 0.8 broadcast_in_dim.4.volb
  1.4 0.0 copy-start
  1.5 0.7 copy-done
  2.1 170.7 %shard_map.68 = (f32[512,1024]{1,0:T(8,128)}, bf16[512,1024]{1,0:T(8,128)(2,1)S(1)}) custom-call(bf16[512,1024]{1,0:T(8,128)(2,1)} %s.1, f32[512,128]{1,0:T(8,128)S(1)} %broadcast_in_dim.4.volb, bf16[1024,512]{1,0:T(8,128)(2,1)} %v.1, f32[1,512]{1,0:T(1,128)S(1)} %bitcast.1, bf16[512,1024]{1,0:T(8,128)(2,1)} %w.1), custom_call_target="tpu_custom_call" | custom-call | tf_op jit(solution)/shard_map/pallas_call | solution.py:365
  172.8 3.2 %copy.9 = f32[512,1024]{1,0:T(8,128)} copy(f32[512,1024]{1,0:T(8,128)} %get-tuple-element.4) | data formatting | bytes 4194304
  176.0 1.0 copy.10
Async XLA Ops:
  1.4 0.7 copy-start

commit v3 on v2

--- a/solution.py
+++ b/solution.py
@@ -10,6 +10,7 @@
 F32, BF16 = jnp.float32, jnp.bfloat16
 MESH = pl.DeviceIdType.MESH
 CHUNKS = 4
+LAG = 2
 
 
 def shards_xla(snapshots, cell_volume, mode_vectors, mode_scale, interp_weights):
@@ -46,8 +47,8 @@
 
 def kernel(
     C, Z, total, s, volb, v, scale, w, gram, fields,
-    sg, sp, volp, wf, gsend, grecv, mpart, mrecv, mg, mgp, dm, csend, crecv, cb, ksend, krecv, kg,
-    loc_sem, ps_sem, pr_sem, xs_sem, xr_sem, zs_sem, zr_sem, gs_sem, gr_sem,
+    sg, sp, volp, wf, gsend, grecv, rrecv, mpart, mrecv, mg, mgp, dm, csend, crecv, cb, ksend, krecv, kg,
+    loc_sem, ps_sem, pr_sem, xs_sem, xr_sem, zs_sem, zr_sem, gs_sem, gr_sem, fs_sem, fr_sem,
     ms_sem, mr_sem, as_sem, ar_sem, cs_sem, cr_sem, bs_sem, br_sem,
     ks_sem, kr_sem, ls_sem, lr_sem,
 ):
@@ -141,6 +142,33 @@
             gsend.at[b, h], grecv.at[p, h], gs_sem.at[b, h], gr_sem.at[p, h], 2 * b + k, z
         )
 
+    def apart(b):
+        return jnp.where(p // 2 == b // 2, 0, 2) + jnp.where(p % 2 == b % 2, 0, 1)
+
+    def flip(b, d):
+        row = 1 - b // 2 if d == 2 else b // 2
+        col = 1 - b % 2 if d == 1 else b % 2
+        return 2 * row + col
+
+    def relays(b, h):
+        odd = h % 2 == 1
+        return (odd & (apart(b) == 1)) | ((h % 2 == 0) & (apart(b) == 2))
+
+    def passes(b, h):
+        return (b != p) & ((((h % 2) == 0) & (apart(b) == 1)) | (((h % 2) == 1) & (apart(b) == 2)))
+
+    def across_send(b, h):
+        to = jnp.where(h % 2 == 1, flip(b, 1), flip(b, 2))
+        return remote(
+            gsend.at[b, h], rrecv.at[b, h], fs_sem.at[b, h], fr_sem.at[b, h], 2 * to + k, z
+        )
+
+    def across_wait(b, h):
+        return remote(
+            gsend.at[b, h], rrecv.at[b, h], fs_sem.at[b, h], fr_sem.at[b, h],
+            2 * other(p, 1, groups) + k, z,
+        )
+
     def gram_term(b, h):
         term = lax.dot_general(
             sg[b, h], wf[...], (((0,), (0,)), ((), ())), preferred_element_type=F32
@@ -153,11 +181,38 @@
         @pl.when(b != p)
         def _():
             gsend[b, h] = term.astype(BF16)
+
+        @pl.when(apart(b) == 3)
+        def _():
+            across_send(b, h).start()
+
+        @pl.when(passes(b, h))
+        def _():
             gram_send(b, h).start()
+
+    def relay(b, h):
+        @pl.when(relays(b, h))
+        def _():
+            across_wait(b, h).wait_recv()
+            gsend[b, h] = (gsend[b, h].astype(F32) + rrecv[b, h].astype(F32)).astype(BF16)
+            gram_send(b, h).start()
+
+    def relay_event(e):
+        @pl.when(e >= 0)
+        def _():
+            t, h = e // CHUNKS, e % CHUNKS
+            for side in (0, 1):
+                b = z - t if side == 0 else z + t
+                there = (b >= 0) if side == 0 else (b < Z) & (t > 0)
+
+                @pl.when(there)
+                def _():
+                    relay(b, h)
 
     @pl.loop(0, CHUNKS)
     def _(h):
         gram_term(z, h)
+        relay_event(h - LAG)
 
     acc = mpart[shape_rows(z), :]
     for d in range(1, Z):
@@ -193,6 +248,7 @@
         @pl.loop(0, CHUNKS)
         def _(h):
             hop(t, h)
+            relay_event(t * CHUNKS + h - LAG)
 
     hops(1)
 
@@ -281,6 +337,9 @@
     for t in range(3, Z):
         hops(t)
 
+    for e in range(Z * CHUNKS - LAG, Z * CHUNKS):
+        relay_event(jnp.int32(e))
+
     new = ksend[c].astype(F32)
     for d in range(1, C):
         q = other(c, d, C)
@@ -298,8 +357,8 @@
     def _(h):
         at = pl.ds(pl.multiple_of(h * cw, cw), cw)
         acc = gram[at, :]
-        for d in range(1, groups):
-            q = other(p, d, groups)
+        for d in (1, 2):
+            q = flip(p, d)
             remote(
                 gsend.at[q, h], grecv.at[q, h], gs_sem.at[q, h], gr_sem.at[q, h], 2 * q + k, z
             ).wait_recv()
@@ -347,8 +406,9 @@
             def _():
                 chain(1, b, h).wait_send()
 
-        for d in range(1, groups):
-            gram_send(other(p, d, groups), h).wait_send()
+        for d in (1, 2):
+            gram_send(flip(p, d), h).wait_send()
+        across_send(flip(flip(p, 1), 2), h).wait_send()
 
 
 def shards_kernel(snapshots, cell_volume, mode_vectors, mode_scale, interp_weights):
@@ -377,6 +437,7 @@
             pltpu.VMEM((2 * rows, cols), BF16),
             pltpu.VMEM((groups, CHUNKS, cw, cols), BF16),
             pltpu.VMEM((groups, CHUNKS, cw, cols), BF16),
+            pltpu.VMEM((groups, CHUNKS, cw, cols), BF16),
             pltpu.VMEM((rows, modes), F32),
             pltpu.VMEM((Z, rows // Z, modes), F32),
             pltpu.VMEM((rows, modes), BF16),
@@ -392,6 +453,7 @@
             dma((3,)), dma((3,)),
             dma((2, Z, CHUNKS)), dma((Z, CHUNKS)),
             dma((groups, CHUNKS)), dma((groups, CHUNKS)),
+            dma((groups, CHUNKS)), dma((groups, CHUNKS)),
             dma((Z,)), dma((Z,)), dma((Z,)), dma((Z,)),
             dma((1,)), dma((groups,)),
             dma((2,)), dma((1,)),
@@ -408,7 +470,7 @@
     rows, cols = snapshots.shape
     modes = mode_vectors.shape[1]
     fits = (
-        C == 2 * Z
+        C == 2 * Z == 8
         and cols % (2 * 128 * CHUNKS) == 0
         and rows % (16 * Z) == 0
         and modes % (16 * C) == 0

time: 177 us -> 173 us (0.977)
  Pallas kernels: 171 us -> 167 us
    pallas_call x1, Pallas kernels: 171 us -> 167 us  [shards_kernel(): pl.pallas_call(functools.partial(kernel, C, Z, rows * C), out_shape=(jax....]
where the time goes in v3:
time: 173 us
  Pallas kernels  167 us (97%)
  local copies, waits for them, and re-layouts  5.61 us (3%)
    pallas_call x1, Pallas kernels, shards_kernel(): pl.pallas_call(functools.partial(kernel, C, Z, rows * C), out_shape=(jax....  167 us
    unnamed x4, local copies, waits for them, and re-layouts  4.81 us

profile of v3, /device:TPU:25, one launch (start us, length us, event | category | flops | bytes accessed | tf_op | source)
XLA Modules:
  0.0 172.8 jit_solution(776014301335765549)
XLA Ops:
  0.6 0.8 broadcast_in_dim.4.volb
  1.4 0.0 copy-start
  1.5 0.7 copy-done
  2.1 166.6 %shard_map.68 = (f32[512,1024]{1,0:T(8,128)}, bf16[512,1024]{1,0:T(8,128)(2,1)S(1)}) custom-call(bf16[512,1024]{1,0:T(8,128)(2,1)} %s.1, f32[512,128]{1,0:T(8,128)S(1)} %broadcast_in_dim.4.volb, bf16[1024,512]{1,0:T(8,128)(2,1)} %v.1, f32[1,512]{1,0:T(1,128)S(1)} %bitcast.1, bf16[512,1024]{1,0:T(8,128)(2,1)} %w.1), custom_call_target="tpu_custom_call" | custom-call | tf_op jit(solution)/shard_map/pallas_call | solution.py:425
  168.7 3.2 %copy.9 = f32[512,1024]{1,0:T(8,128)} copy(f32[512,1024]{1,0:T(8,128)} %get-tuple-element.4) | data formatting | bytes 4194304
  171.9 1.0 copy.10
Async XLA Ops:
  1.4 0.7 copy-start

commit v4 on v3

--- a/solution.py
+++ b/solution.py
@@ -120,7 +120,7 @@
         to = jnp.minimum(z + 1, Z - 1) if side == 0 else jnp.maximum(z - 1, 0)
         return remote(sg.at[b, h], sg.at[b, h], zs_sem.at[side, b, h], zr_sem.at[b, h], c, to)
 
-    for h in range(CHUNKS):
+    def own_send(h):
         local_copy(h).wait()
         mate_copy(h).wait_recv()
 
@@ -131,6 +131,9 @@
         @pl.when(z > 0)
         def _():
             chain(1, z, h).start()
+
+    for h in range(CHUNKS // 2):
+        own_send(h)
 
     wf[mine, :] = (s[...].astype(F32) * volb[:, :1]).astype(BF16)
     vol_copy.wait_recv()
@@ -209,24 +212,28 @@
                 def _():
                     relay(b, h)
 
+
+    acc = mpart[shape_rows(z), :]
+    for d in range(1, Z):
+        q = other(z, d, Z)
+        remote(mpart.at[shape_rows(z)], mrecv.at[q], ms_sem.at[q], mr_sem.at[q], c, q).wait_recv()
+        acc = acc + mrecv[q]
+    mg[shape_rows(z), :] = acc.astype(BF16)
+
+    def shape_share(d, b):
+        t = other(z, d, Z)
+        return remote(mg.at[shape_rows(b)], mg.at[shape_rows(b)], as_sem.at[t], ar_sem.at[b], c, t)
+
+    for d in range(1, Z):
+        shape_share(d, z).start()
+
+    for h in range(CHUNKS // 2, CHUNKS):
+        own_send(h)
+
     @pl.loop(0, CHUNKS)
     def _(h):
         gram_term(z, h)
         relay_event(h - LAG)
-
-    acc = mpart[shape_rows(z), :]
-    for d in range(1, Z):
-        q = other(z, d, Z)
-        remote(mpart.at[shape_rows(z)], mrecv.at[q], ms_sem.at[q], mr_sem.at[q], c, q).wait_recv()
-        acc = acc + mrecv[q]
-    mg[shape_rows(z), :] = acc.astype(BF16)
-
-    def shape_share(d, b):
-        t = other(z, d, Z)
-        return remote(mg.at[shape_rows(b)], mg.at[shape_rows(b)], as_sem.at[t], ar_sem.at[b], c, t)
-
-    for d in range(1, Z):
-        shape_share(d, z).start()
 
     def hop(t, h):
         for side in (0, 1):
@@ -244,13 +251,11 @@
 
                 gram_term(b, h)
 
-    def hops(t):
-        @pl.loop(0, CHUNKS)
+    def hops(t, first=0, last=CHUNKS):
+        @pl.loop(first, last)
         def _(h):
             hop(t, h)
             relay_event(t * CHUNKS + h - LAG)
-
-    hops(1)
 
     for d in range(1, Z):
         shape_share(d, other(z, d, Z)).wait_recv()
@@ -265,9 +270,9 @@
     def coeff_send():
         return remote(csend, crecv.at[p], cs_sem.at[0], cr_sem.at[p], 2 * z + k, z)
 
-    def coeff_share(side):
-        to = jnp.minimum(z + 1, Z - 1) if side == 0 else jnp.maximum(z - 1, 0)
-        return remote(cb, cb, bs_sem.at[side], br_sem.at[0], c, to)
+    def coeff_share(d):
+        t = other(z, d, Z)
+        return remote(cb, cb, bs_sem.at[t], br_sem.at[0], c, t)
 
     @pl.loop(0, CHUNKS)
     def _(h):
@@ -288,8 +293,7 @@
     def _():
         coeff_send().start()
 
-    if Z > 2:
-        hops(2)
+    hops(1)
 
     @pl.when(diagonal)
     def _():
@@ -302,30 +306,15 @@
             total_c = total_c + crecv[q].astype(F32)
         cb[...] = (total_c * (scale[...] * (1.0 / total))).astype(BF16)
 
-        @pl.when(z < Z - 1)
-        def _():
-            coeff_share(0).start()
-
-        @pl.when(z > 0)
-        def _():
-            coeff_share(1).start()
-
-    @pl.when(z > p)
-    def _():
-        coeff_share(0).wait_recv()
-
-        @pl.when(z < Z - 1)
-        def _():
-            coeff_share(0).start()
-
-    @pl.when(z < p)
+        for d in range(1, Z):
+            coeff_share(d).start()
+
+    hops(2)
+
+    @pl.when(p != z)
     def _():
         coeff_share(1).wait_recv()
 
-        @pl.when(z > 0)
-        def _():
-            coeff_share(1).start()
-
     def new_send(t):
         return remote(ksend.at[t], krecv.at[c], ks_sem.at[t], kr_sem.at[c], t, z)
 
@@ -334,11 +323,7 @@
     for d in range(1, C):
         new_send(other(c, d, C)).start()
 
-    for t in range(3, Z):
-        hops(t)
-
-    for e in range(Z * CHUNKS - LAG, Z * CHUNKS):
-        relay_event(jnp.int32(e))
+    hops(3, 0, CHUNKS // 2)
 
     new = ksend[c].astype(F32)
     for d in range(1, C):
@@ -352,6 +337,10 @@
 
     for d in range(1, C):
         new_share(other(c, d, C), c).start()
+
+    hops(3, CHUNKS // 2)
+    for e in range(Z * CHUNKS - LAG, Z * CHUNKS):
+        relay_event(jnp.int32(e))
 
     @pl.loop(0, CHUNKS)
     def _(h):
@@ -387,13 +376,10 @@
     def _():
         coeff_send().wait_send()
 
-    @pl.when((z >= p) & (z < Z - 1))
+    @pl.when(diagonal)
     def _():
-        coeff_share(0).wait_send()
-
-    @pl.when((z <= p) & (z > 0))
-    def _():
-        coeff_share(1).wait_send()
+        for d in range(1, Z):
+            coeff_share(d).wait_send()
 
     @pl.loop(0, CHUNKS)
     def _(h):
@@ -456,7 +442,7 @@
             dma((groups, CHUNKS)), dma((groups, CHUNKS)),
             dma((Z,)), dma((Z,)), dma((Z,)), dma((Z,)),
             dma((1,)), dma((groups,)),
-            dma((2,)), dma((1,)),
+            dma((Z,)), dma((1,)),
             dma((C,)), dma((C,)), dma((C,)), dma((C,)),
         ],
         compiler_params=pltpu.CompilerParams(

time: 173 us -> 173 us (level)
  no operation moved by 1% of the time
where the time goes in v4:
time: 173 us
  Pallas kernels  167 us (97%)
  local copies, waits for them, and re-layouts  5.61 us (3%)
    pallas_call x1, Pallas kernels, shards_kernel(): pl.pallas_call(functools.partial(kernel, C, Z, rows * C), out_shape=(jax....  167 us
    unnamed x4, local copies, waits for them, and re-layouts  4.81 us

profile of v4, /device:TPU:25, one launch (start us, length us, event | category | flops | bytes accessed | tf_op | source)
XLA Modules:
  0.0 173.1 jit_solution(8213663142927851064)
XLA Ops:
  0.6 0.8 broadcast_in_dim.4.volb
  1.4 0.0 copy-start
  1.5 0.7 copy-done
  2.1 166.9 %shard_map.68 = (f32[512,1024]{1,0:T(8,128)}, bf16[512,1024]{1,0:T(8,128)(2,1)S(1)}) custom-call(bf16[512,1024]{1,0:T(8,128)(2,1)} %s.1, f32[512,128]{1,0:T(8,128)S(1)} %broadcast_in_dim.4.volb, bf16[1024,512]{1,0:T(8,128)(2,1)} %v.1, f32[1,512]{1,0:T(1,128)S(1)} %bitcast.1, bf16[512,1024]{1,0:T(8,128)(2,1)} %w.1), custom_call_target="tpu_custom_call" | custom-call | tf_op jit(solution)/shard_map/pallas_call | solution.py:411
  169.0 3.2 %copy.9 = f32[512,1024]{1,0:T(8,128)} copy(f32[512,1024]{1,0:T(8,128)} %get-tuple-element.4) | data formatting | bytes 4194304
  172.2 1.0 copy.10
Async XLA Ops:
  1.4 0.7 copy-start
